TPU v7x, 32 devices: a whole 2x2x4 slice. The times are simulated.
32 devices in a mesh: obs: 4 (over y, core), flux: 8 (over z, x).
Axes of the slice: x: 2, y: 2, z: 4, core: 2. Of those that a mesh axis runs over, the one named last changes fastest.
Arguments:
- jacobian: bfloat16 [512, 8192], P('obs', 'flux'), may hold values from -0.0625 to 0.0625
- probes: bfloat16 [2, 8192, 128], P(None, 'flux'), may hold values from -6 to 6
- prior_std: float32 [8192], P('flux'), may hold values from 0.5 to 2
- obs_weight: float32 [512], P('obs'), may hold values from 0.25 to 4
Outputs:
- sketch: float32 [8192, 256], P(('flux', 'obs'))
- basis_out: float32 [8192, 256], P(('flux', 'obs'))
All inputs are finite; a program needn't handle non-finite values.
Results may differ from a plain program's by a relative error of at most 0.005.
Values may be sent and summed in bfloat16 or wider, within the bound.
A program may use at most 64 MiB of HBM per device.

v0:
```python
import math

import jax
import jax.numpy as jnp
from jax import lax
from jax.sharding import PartitionSpec as P


def body(jacobian, probes, prior_std, obs_weight):
    block_count, flux_local, probe_count = probes.shape
    scaled = (probes.astype(jnp.float32) * prior_std[None, :, None]).astype(jnp.bfloat16)
    portion = flux_local // lax.axis_size("obs")
    offset = lax.axis_index("obs") * portion
    local_std = lax.dynamic_slice_in_dim(prior_std, offset, portion)
    stacked = jnp.transpose(scaled, (1, 0, 2)).reshape(flux_local, block_count * probe_count)
    forward = lax.psum(jnp.dot(jacobian, stacked, preferred_element_type=jnp.float32), "flux")
    weighted = (forward * obs_weight[:, None]).astype(jnp.bfloat16)
    adjoint = lax.psum_scatter(
        lax.dot_general(
            jacobian, weighted, (((0,), (0,)), ((), ())), preferred_element_type=jnp.float32
        ),
        "obs",
        scatter_dimension=0,
        tiled=True,
    )
    sketch = adjoint * local_std[:, None]
    gram_matrix = lax.psum(
        jnp.dot(
            sketch.T, sketch, precision=lax.Precision.HIGHEST, preferred_element_type=jnp.float32
        ),
        ("obs", "flux"),
    )
    factor = jnp.linalg.cholesky(gram_matrix)
    scale_root = math.sqrt(flux_local * lax.axis_size("flux"))
    basis_out = jax.scipy.linalg.solve_triangular(factor, sketch.T, lower=True).T * scale_root
    return (sketch, basis_out)


def solution(mesh):
    in_specs = (P("obs", "flux"), P(None, "flux", None), P("flux"), P("obs"))
    out_specs = (P(("flux", "obs"), None), P(("flux", "obs"), None))
    return jax.shard_map(body, mesh=mesh, in_specs=in_specs, out_specs=out_specs, check_vma=False)
```

profile of v0, /device:TPU:1, one launch (start us, length us, event | category | flops | bytes accessed | tf_op | source)
XLA Modules:
  0.0 312.4 jit_solution(5051485426730443432)
XLA Ops:
  7.2 1.3 copy.10
  8.5 0.1 multiply_convert_fusion
  8.7 1.0 convolution_bitcast_fusion.1
  9.6 0.0 reduce-scatter.2.cloned.1.call-start
  9.7 73.0 %all-reduce.4.cloned.1.call-done = f32[128,256]{0,1:T(8,128)} async-done(((f32[128,256]{0,1:T(8,128)}), f32[128,256]{0,1:T(8,128)}) %all-reduce.4.cloned.1.call-update) | async-done | bytes 131088 | tf_op jit(solution)/shard_map/psum | solution.py:16
  82.7 2.2 convolution_bitcast_fusion
  84.9 0.0 all-reduce.6.cloned.1.call-start
  84.9 0.1 dynamic_slice.3
  85.0 25.8 %reduce-scatter.2.cloned.1.call-done = f32[256,256]{0,1:T(8,128)} async-done(((f32[1024,256]{0,1:T(8,128)}), f32[256,256]{0,1:T(8,128)}) %reduce-scatter.2.cloned.1.call-update) | async-done | bytes 262160 | tf_op jit(solution)/shard_map/reduce_scatter | solution.py:18
  110.8 1.0 broadcast_multiply_fusion
  111.8 0.8 copy.13
  112.6 1.1 fusion.11
  113.8 0.9 copy-done.2
  114.7 128.2 %all-reduce.6.cloned.1.call-done = f32[256,256]{0,1:T(8,128)} async-done(((f32[256,256]{0,1:T(8,128)}), f32[256,256]{0,1:T(8,128)}) %all-reduce.6.cloned.1.call-update) | async-done | bytes 262160 | tf_op jit(solution)/shard_map/psum | solution.py:27
  243.0 1.1 copy.12
  244.2 11.7 %cholesky.50 = f32[128,128]{1,0:T(8,128)S(1)} custom-call(f32[128,128]{1,0:T(8,128)S(1)} %cholesky.118), custom_call_target="Cholesky" | custom-call | tf_op jit(solution)/shard_map/jit(cholesky)/cholesky | solution.py:33
  256.0 9.8 %custom-call.15 = f32[1,128,128]{1,2,0:T(8,128)S(1)} custom-call(f32[1,128,128]{2,1,0:T(8,128)S(1)} %get-tuple-element.27), custom_call_target="InvertDiagBlocksLowerTriangular" | custom-call | tf_op jit(solution)/shard_map/jit(cholesky)/cholesky | solution.py:33
  265.8 0.2 constant_dynamic-update-slice_fusion.1
  266.0 0.3 convolution_subtract_fusion.1
  266.3 11.7 %cholesky.105 = f32[128,128]{1,0:T(8,128)S(1)} custom-call(f32[128,128]{1,0:T(8,128)S(1)} %convolution_subtract_fusion.1), custom_call_target="Cholesky" | custom-call | tf_op jit(solution)/shard_map/jit(cholesky)/cholesky | solution.py:33
  278.0 0.7 compare_reduce_fusion
  280.1 0.1 triangular_solve.57
  280.2 4.2 %while.1 = (s32[]{:T(128)}, f32[256,256]{1,0:T(8,128)S(1)}, s32[2,2]{1,0:T(2,128)S(1)}, f32[2,128,128]{2,1,0:T(8,128)S(1)}, s32[]{:T(128)}) while((s32[]{:T(128)}, f32[256,256]{1,0:T(8,128)S(1)}, s32[2,2]{1,0:T(2,128)S(1)}, f32[2,128,128]{2,1,0:T(8,128)S(1)}, s32[]{:T(128)}) %tuple.29), condition=%wide.while_cond, body=%wide.while_body.sunk | while | flops 2 | bytes 131189 | solution.py:35
  280.3 0.6 fusion.23
  280.9 1.4 bitcast_dynamic-update-slice_fusion.2
  282.4 0.6 fusion.23
  283.0 1.4 bitcast_dynamic-update-slice_fusion.2
  284.4 19.7 %custom-call.16 = f32[2,128,128]{1,2,0:T(8,128)S(1)} custom-call(f32[2,128,128]{2,1,0:T(8,128)S(1)} %get-tuple-element.9), custom_call_target="InvertDiagBlocksLowerTriangular" | custom-call | tf_op jit(solution)/shard_map/jit(_solve_triangular)/triangular_solve | solution.py:35
  304.1 0.3 fusion.2
  304.4 0.3 convolution_subtract_fusion
  304.7 0.3 fusion.5
  305.1 0.8 copy.14
  (25 shorter events, 0.3 us)
Async XLA Ops:
  7.2 1.5 copy-start
  7.2 1.3 copy-start.3
  7.2 75.5 %all-reduce.4.cloned.1.call-start = ((), (), s32[]{:S(2)}) async-start(), calls=%async_computation.1 | async-start | bytes 262144 | tf_op jit(solution)/shard_map/psum | solution.py:16
  9.6 73.0 %copy-start.4 = (f32[128]{0:T(128)S(1)}, f32[128]{0:T(128)}, u32[]{:S(2)}) copy-start(f32[128]{0:T(128)} %param.7) | copy-start | bytes 1540
  9.6 101.2 %reduce-scatter.2.cloned.1.call-start = ((), (), s32[]{:S(2)}) async-start(), calls=%async_computation.2 | async-start | bytes 1310720 | tf_op jit(solution)/shard_map/reduce_scatter | solution.py:18
  84.9 158.1 %all-reduce.6.cloned.1.call-start = ((), (), s32[]{:S(2)}) async-start(), calls=%async_computation.3 | async-start | bytes 524288 | tf_op jit(solution)/shard_map/psum | solution.py:27
  113.7 0.9 copy-start.2
  243.0 1.2 copy-start.1
Sparse Core Ops, SparseCore 0:
  11.9 70.6 all-reduce.3
  85.2 25.5 reduce-scatter.1
  116.9 126.0 all-reduce.5
where the time goes:
time: 314 us; the launch traced here: 312 us
  waiting for transfers between devices  227 us (72%)
  other arithmetic  54.9 us (17%)
  between operations  15.3 us (5%)
  local copies, waits for them, and re-layouts  9.28 us (3%)
  matrix products  5.61 us (2%)
    psum x1, waiting for transfers between devices, body(): lax.psum(jnp.dot(sketch.T, sketch, precision=lax.Precision.HIGHEST, prefe...  128 us
    psum x1, waiting for transfers between devices, body(): lax.psum(jnp.dot(jacobian, stacked, preferred_element_type=jnp.float32),...  73 us
    another operation x6, other arithmetic, body(): factor = jnp.linalg.cholesky(gram_matrix)  34 us
    reduce_scatter x1, waiting for transfers between devices, body(): lax.psum_scatter(lax.dot_general(jacobian, weighted, (((0,), (0,)), ((),...  25.8 us
    another operation x3, other arithmetic, body(): jax.scipy.linalg.solve_triangular(factor, sketch.T, lower=True)  19.7 us
  transfers between devices with their start and end apart: 3, of which 3 were waited for; matrix products, arithmetic and copies ran while one was open for 0% of the time, Pallas kernels for 0%

commit v1 on v0

v1 whole, which is shorter than its diff:
```python
import functools
import math

import jax
import jax.numpy as jnp
from jax import lax
from jax.experimental import pallas as pl
from jax.experimental.pallas import tpu as pltpu
from jax.sharding import PartitionSpec as P

MESH = pl.DeviceIdType.MESH
HIGHEST = lax.Precision.HIGHEST
F32 = jnp.float32
BF16 = jnp.bfloat16
LANES = 128
PANEL = 32


def each(lower, upper, step):
    if upper - lower <= 16:
        for value in range(lower, upper):
            step(value)
    else:
        lax.fori_loop(lower, upper, lambda value, carry: (step(value), carry)[1], 0)


def only(condition, step):
    if condition is True:
        step()
    else:
        pl.when(condition)(step)


def wait_bytes(ref, sem):
    pltpu.make_async_copy(ref, ref, sem).wait()


def column(row):
    return jnp.broadcast_to(row, (LANES, LANES)).T


def factor_inverse(work, width):
    for start in range(0, width, PANEL):
        stop = start + PANEL
        left = start // LANES * LANES
        right = width + (stop + LANES - 1) // LANES * LANES
        rows = work[start:stop, left:right]
        index = lax.broadcasted_iota(jnp.int32, (PANEL, 1), 0)
        diagonal = jnp.zeros((PANEL, 1), F32)
        for k in range(PANEL):
            at = start - left + k
            pivot_row = rows[k : k + 1, :]
            multiplier = rows[:, at : at + 1]
            pivot = multiplier[k : k + 1, :]
            diagonal = jnp.where(index == k, pivot, diagonal)
            scaled = jnp.where(index > k, multiplier, 0.0) * (1.0 / pivot)
            rows = rows - scaled * pivot_row
        rows = rows * (1.0 / jnp.sqrt(diagonal))
        work[start:stop, left:right] = rows
        if stop < width:
            update = lax.dot_general(
                rows[:, : width - left],
                rows,
                (((0,), (0,)), ((), ())),
                precision=HIGHEST,
                preferred_element_type=F32,
            )
            work[stop:width, left:right] = work[stop:width, left:right] - update[stop - left :, :]


def kernel(
    sizes, jac, probes, std, weight, sketch_out, basis_out,
    std_col, weight_col, stacked, jt, jrecv, fsend, frecv, wbuf,
    gsend, gpair, gchunk, grecv, gfull, work, send_sems, recv_sems,
):
    n_obs, n_flux, scale = sizes
    blocks, flux_local, probe_count = probes.shape
    obs_local = jac.shape[0]
    width = blocks * probe_count
    portion = flux_local // n_obs
    n_y = n_obs // 2
    chips = n_y * n_flux
    w_owners, w_rows = fsend.shape[0], fsend.shape[1]
    g_owners = gsend.shape[1]

    o, f = lax.axis_index("obs"), lax.axis_index("flux")
    core, y = lax.rem(o, 2), o // 2
    chip = y * n_flux + f
    partner = (o + 1 - 2 * core, f)
    w_mine = True if w_owners == n_flux else f < w_owners
    g_mine = True if g_owners == chips else chip < g_owners

    def on_chip(step, c):
        other = lax.rem(chip + step, chips)
        return other, ((other // n_flux) * 2 + c, lax.rem(other, n_flux))

    barrier = pltpu.get_barrier_semaphore()

    def greet(step):
        _, device = on_chip(step, core)
        pl.semaphore_signal(barrier, inc=1, device_id=device, device_id_type=MESH)

    def greet_other(step):
        _, device = on_chip(step, 1 - core)
        pl.semaphore_signal(barrier, inc=1, device_id=device, device_id_type=MESH)

    each(1, chips, greet)
    each(0, chips, greet_other)

    for s in range(flux_local // LANES):
        part = slice(s * LANES, (s + 1) * LANES)
        std_col[part, :] = column(std[:, part])
    for s in range(obs_local // LANES):
        part = slice(s * LANES, (s + 1) * LANES)
        weight_col[part, :] = column(weight[:, part])
    for b in range(blocks):
        stacked[:, b * probe_count : (b + 1) * probe_count] = (
            probes[b].astype(F32) * std_col[...]
        ).astype(BF16)
    partial = jnp.dot(jac[...], stacked[...], preferred_element_type=F32)
    fsend[...] = partial.reshape(w_owners, w_rows, width)
    jt[...] = jac[...].T.reshape(n_obs, portion, obs_local)

    pl.semaphore_wait(barrier, 2 * chips - 1)

    def send(src, dst, number, device):
        copy = pltpu.make_async_remote_copy(
            src_ref=src, dst_ref=dst, send_sem=send_sems.at[number],
            recv_sem=recv_sems.at[number], device_id=device, device_id_type=MESH,
        )
        copy.start()
        return copy

    def send_forward(step):
        other = lax.rem(f + step, n_flux)
        only(
            True if w_owners == n_flux else other < w_owners,
            lambda: send(fsend.at[other], frecv.at[f], 0, (o, other)) and None,
        )

    each(1, n_flux, send_forward)

    def send_jacobian(step):
        other = lax.rem(o + step, n_obs)
        send(jt.at[other], jrecv.at[core, y], 1, (other, f))

    each(1, n_obs, send_jacobian)
    jrecv[core, y] = jt[o]

    def weigh():
        frecv[f] = fsend[f]
        wait_bytes(frecv.at[pl.ds(0, n_flux - 1)], recv_sems.at[0])
        rows = jnp.sum(frecv[...], axis=0)
        at = pl.ds(pl.multiple_of(f * w_rows, w_rows), w_rows)
        factor = jnp.concatenate([weight_col[at, :]] * (width // LANES), axis=1)
        mine = y * w_owners + f
        wbuf[core, mine] = (rows * factor).astype(BF16)

        def share(step):
            _, device = on_chip(step, core)
            send(wbuf.at[core, mine], wbuf.at[core, mine], 2, device)

        each(1, chips, share)

    only(w_mine, weigh)
    w_total = n_y * w_owners
    if w_mine is True:
        wait_bytes(wbuf.at[core, pl.ds(0, w_total - 1)], recv_sems.at[2])
    else:
        pl.when(w_mine)(lambda: wait_bytes(wbuf.at[core, pl.ds(0, w_total - 1)], recv_sems.at[2]))
        pl.when(f >= w_owners)(lambda: wait_bytes(wbuf.at[core], recv_sems.at[2]))
    across = send(wbuf.at[core], wbuf.at[core], 3, partner)

    wait_bytes(jt.at[pl.ds(0, n_obs - 1)], recv_sems.at[1])

    def adjoint(c):
        total = jnp.zeros((portion, width), F32)
        for row in range(n_y):
            piece = wbuf[c, row * w_owners : (row + 1) * w_owners].reshape(obs_local, width)
            total = total + jnp.dot(jrecv[c, row], piece, preferred_element_type=F32)
        return total

    own_half = adjoint(core)
    across.wait_recv()
    total = own_half + adjoint(1 - core)
    at = pl.ds(pl.multiple_of(o * portion, portion), portion)
    sketch = total * jnp.concatenate([std_col[at, :]] * (width // LANES), axis=1)
    sketch_out[...] = sketch
    gram = lax.dot_general(
        sketch, sketch, (((0,), (0,)), ((), ())), precision=HIGHEST, preferred_element_type=F32
    )
    gsend[...] = gram.reshape(gsend.shape)

    pair = send(gsend.at[1 - core], gpair, 4, partner)
    pair.wait_recv()
    gchunk[...] = gsend[core] + gpair[...]

    def send_gram(step):
        other, device = on_chip(step, core)
        only(
            True if g_owners == chips else other < g_owners,
            lambda: send(gchunk.at[other], grecv.at[chip], 5, device) and None,
        )

    each(1, chips, send_gram)

    def total_gram():
        grecv[chip] = gchunk[chip]
        wait_bytes(grecv.at[pl.ds(0, chips - 1)], recv_sems.at[5])
        gfull[core, chip] = jnp.sum(grecv[...], axis=0)

        def share(step):
            _, device = on_chip(step, core)
            send(gfull.at[core, chip], gfull.at[core, chip], 6, device)

        each(1, chips, share)

    only(g_mine, total_gram)
    if g_mine is True:
        wait_bytes(gfull.at[core, pl.ds(0, g_owners - 1)], recv_sems.at[6])
    else:
        pl.when(g_mine)(lambda: wait_bytes(gfull.at[core, pl.ds(0, g_owners - 1)], recv_sems.at[6]))
        pl.when(chip >= g_owners)(lambda: wait_bytes(gfull.at[core], recv_sems.at[6]))
    gacross = send(gfull.at[core], gfull.at[core], 7, partner)
    gacross.wait_recv()

    work[:, :width] = gfull[...].reshape(width, width)
    work[:, width:] = (
        lax.broadcasted_iota(jnp.int32, (width, width), 0)
        == lax.broadcasted_iota(jnp.int32, (width, width), 1)
    ).astype(F32)
    factor_inverse(work, width)
    basis = lax.dot_general(
        sketch_out[...], work[:, width:], (((1,), (1,)), ((), ())),
        precision=HIGHEST, preferred_element_type=F32,
    )
    basis_out[...] = basis * scale

    if w_mine is True:
        wait_bytes(fsend.at[pl.ds(0, w_owners - 1)], send_sems.at[0])
        wait_bytes(grecv.at[pl.ds(0, 0 + chips - 1)], send_sems.at[5])
    else:
        pl.when(w_mine)(lambda: wait_bytes(fsend.at[pl.ds(0, w_owners - 1)], send_sems.at[0]))
        pl.when(f >= w_owners)(lambda: wait_bytes(fsend, send_sems.at[0]))
        pl.when(g_mine)(lambda: wait_bytes(gchunk.at[pl.ds(0, g_owners - 1)], send_sems.at[5]))
        pl.when(chip >= g_owners)(lambda: wait_bytes(gchunk, send_sems.at[5]))
    wait_bytes(jt.at[pl.ds(0, n_obs - 1)], send_sems.at[1])

    def w_sent():
        each(1, chips, lambda step: wait_bytes(wbuf.at[core, 0], send_sems.at[2]))

    only(w_mine, w_sent)
    across.wait_send()
    pair.wait_send()

    def g_sent():
        each(1, chips, lambda step: wait_bytes(gfull.at[core, 0], send_sems.at[6]))

    only(g_mine, g_sent)
    gacross.wait_send()


def body(jacobian, probes, prior_std, obs_weight):
    blocks, flux_local, probe_count = probes.shape
    obs_local = jacobian.shape[0]
    n_obs, n_flux = lax.axis_size("obs"), lax.axis_size("flux")
    width = blocks * probe_count
    portion = flux_local // n_obs
    chips = n_obs // 2 * n_flux
    w_rows = max(16, obs_local // n_flux)
    w_owners = obs_local // w_rows
    g_rows = max(8, width // 2 // chips)
    g_owners = width // 2 // g_rows
    scale = math.sqrt(flux_local * n_flux)
    vmem = pl.BlockSpec(memory_space=pltpu.VMEM)
    out = jax.ShapeDtypeStruct((portion, width), F32)
    return pl.pallas_call(
        functools.partial(kernel, (n_obs, n_flux, scale)),
        out_shape=(out, out),
        in_specs=[vmem] * 4,
        out_specs=(vmem, vmem),
        scratch_shapes=[
            pltpu.VMEM((flux_local, LANES), F32),
            pltpu.VMEM((obs_local, LANES), F32),
            pltpu.VMEM((flux_local, width), BF16),
            pltpu.VMEM((n_obs, portion, obs_local), BF16),
            pltpu.VMEM((2, n_obs // 2, portion, obs_local), BF16),
            pltpu.VMEM((w_owners, w_rows, width), F32),
            pltpu.VMEM((n_flux, w_rows, width), F32),
            pltpu.VMEM((2, n_obs // 2 * w_owners, w_rows, width), BF16),
            pltpu.VMEM((2, g_owners, g_rows, width), F32),
            pltpu.VMEM((g_owners, g_rows, width), F32),
            pltpu.VMEM((g_owners, g_rows, width), F32),
            pltpu.VMEM((chips, g_rows, width), F32),
            pltpu.VMEM((2, g_owners, g_rows, width), F32),
            pltpu.VMEM((width, 2 * width), F32),
            pltpu.SemaphoreType.DMA((8,)),
            pltpu.SemaphoreType.DMA((8,)),
        ],
        compiler_params=pltpu.CompilerParams(collective_id=0, has_side_effects=True),
    )(jacobian, probes, prior_std.reshape(1, -1), obs_weight.reshape(1, -1))


def solution(mesh):
    in_specs = (P("obs", "flux"), P(None, "flux", None), P("flux"), P("obs"))
    out_specs = (P(("flux", "obs"), None), P(("flux", "obs"), None))
    return jax.shard_map(body, mesh=mesh, in_specs=in_specs, out_specs=out_specs, check_vma=False)
```

time: 314 us -> 61.6 us (0.20)
  waiting for transfers between devices: 227 us -> 0 us
  Pallas kernels: 0 us -> 58.4 us
  other arithmetic: 54.9 us -> 0 us
  between operations: 15.3 us -> 0.65 us
  local copies, waits for them, and re-layouts: 9.28 us -> 2.42 us
  matrix products: 5.61 us -> 0 us
    psum x2 -> x0, waiting for transfers between devices: 201 us -> none  [the longest x1 128 us: body(): lax.psum(jnp.dot(sketch.T, sketch, precision=lax.Precision.HIGHEST, prefe...]
    pallas_call x0 -> x1, Pallas kernels: none -> 58.4 us  [body(): pl.pallas_call(functools.partial(kernel, (n_obs, n_flux, scale)), out_sha...]
    another operation x9 -> x0, other arithmetic: 53.7 us -> none  [the longest x6 34 us: body(): factor = jnp.linalg.cholesky(gram_matrix)]
    reduce_scatter x1 -> x0, waiting for transfers between devices: 25.8 us -> none  [body(): lax.psum_scatter(lax.dot_general(jacobian, weighted, (((0,), (0,)), ((),...]
    dot_general x3 -> x0, matrix products: 4.26 us -> none  [the longest x1 2.18 us: body(): lax.dot_general(jacobian, weighted, (((0,), (0,)), ((), ())), preferred_e...]
    another operation x9 -> x0, local copies, waits for them, and re-layouts: 4.15 us -> none
  transfers between devices with their start and end apart: 3 -> 0, of which waited for: 3 -> 0; matrix products, arithmetic and copies ran while one was open for 0% -> 0% of each run, Pallas kernels for 0% -> 0%
where the time goes in v1:
time: 61.6 us; the launch traced here: 61.5 us
  Pallas kernels  58.4 us (95%)
  local copies, waits for them, and re-layouts  2.42 us (4%)
  between operations  0.65 us (1%)
    pallas_call x1, Pallas kernels, body(): pl.pallas_call(functools.partial(kernel, (n_obs, n_flux, scale)), out_sha...  58.4 us
    unnamed x4, local copies, waits for them, and re-layouts  2.42 us

profile of v1, /device:TPU:1, one launch (start us, length us, event | category | flops | bytes accessed | tf_op | source)
XLA Modules:
  0.0 61.5 jit_solution(6829598843445258390)
XLA Ops:
  0.6 58.4 %shard_map.59 = (f32[256,256]{1,0:T(8,128)}, f32[256,256]{1,0:T(8,128)}) custom-call(bf16[128,1024]{1,0:T(8,128)(2,1)} %jac.1, bf16[2,1024,128]{2,1,0:T(8,128)(2,1)} %probes.1, f32[1,1024]{1,0:T(1,128)} %bitcast.2, f32[1,128]{1,0:T(1,128)} %bitcast.3), custom_call_target="tpu_custom_call" | custom-call | tf_op jit(solution)/shard_map/pallas_call | solution.py:277
  59.0 0.0 copy-start
  59.1 1.7 %copy.8 = f32[256,256]{1,0:T(8,128)} copy(f32[256,256]{1,0:T(8,128)} %get-tuple-element.4) | data formatting | bytes 524288
  60.8 0.0 copy-done
  60.8 0.7 %copy.9 = f32[256,256]{1,0:T(8,128)} copy(f32[256,256]{1,0:T(8,128)S(1)} %copy-done) | data formatting | bytes 524288
Async XLA Ops:
  59.0 1.7 %copy-start = (f32[256,256]{1,0:T(8,128)S(1)}, f32[256,256]{1,0:T(8,128)}, u32[]{:S(2)}) copy-start(f32[256,256]{1,0:T(8,128)} %get-tuple-element.5) | copy-start | bytes 786436

commit v2 on v1

--- a/solution.py
+++ b/solution.py
@@ -13,7 +13,8 @@
 F32 = jnp.float32
 BF16 = jnp.bfloat16
 LANES = 128
-PANEL = 32
+PANEL = 64
+TILE = 8
 
 
 def each(lower, upper, step):
@@ -39,41 +40,79 @@
     return jnp.broadcast_to(row, (LANES, LANES)).T
 
 
+def factor_rows(work, start, stop, width):
+    index = lax.broadcasted_iota(jnp.int32, (TILE, LANES), 0)
+
+    def spread(x, k):
+        return jnp.broadcast_to(x[k : k + 1, :], x.shape)
+
+    def columns(x, at):
+        return [jnp.broadcast_to(x[:, at + j : at + j + 1], (TILE, LANES)) for j in range(TILE)]
+
+    for first in range(start, stop, TILE):
+        left = first // LANES * LANES
+        right = width + left + LANES
+        spans = [slice(s, s + LANES) for s in range(0, right - left, LANES)]
+        top = work[first : first + TILE, left:right]
+        cols = columns(top, first - left)
+        parts = [top[:, span] for span in spans]
+        steps = []
+        diagonal = jnp.ones((TILE, LANES), F32)
+        for k in range(TILE):
+            pivot = spread(cols[k], k)
+            diagonal = jnp.where(index == k, pivot, diagonal)
+            inverse = 1.0 / pivot
+            pivot_row = [spread(part, k) for part in parts]
+            heads = [spread(col, k) for col in cols]
+            steps.append((inverse, pivot_row, heads))
+            if k < TILE - 1:
+                multiplier = jnp.where(index > k, cols[k], 0.0) * inverse
+                for j in range(k + 1, TILE):
+                    cols[j] = cols[j] - multiplier * heads[j]
+                parts = [part - multiplier * row for part, row in zip(parts, pivot_row)]
+        for below in range(first + TILE, stop, TILE):
+            tile = work[below : below + TILE, left:right]
+            lower = columns(tile, first - left)
+            pieces = [tile[:, span] for span in spans]
+            for k, (inverse, pivot_row, heads) in enumerate(steps):
+                multiplier = lower[k] * inverse
+                for j in range(k + 1, TILE):
+                    lower[j] = lower[j] - multiplier * heads[j]
+                pieces = [piece - multiplier * row for piece, row in zip(pieces, pivot_row)]
+            for span, piece in zip(spans, pieces):
+                work[below : below + TILE, left + span.start : left + span.stop] = piece
+        root = 1.0 / jnp.sqrt(diagonal)
+        for span, part in zip(spans, parts):
+            work[first : first + TILE, left + span.start : left + span.stop] = part * root
+
+
+def take_out(work, start, stop, low, high, width):
+    left = low // LANES * LANES
+    right = width + (stop + LANES - 1) // LANES * LANES
+    update = lax.dot_general(
+        work[start:stop, left : (high + LANES - 1) // LANES * LANES],
+        work[start:stop, left:right],
+        (((0,), (0,)), ((), ())),
+        precision=HIGHEST,
+        preferred_element_type=F32,
+    )
+    work[low:high, left:right] = work[low:high, left:right] - update[low - left : high - left, :]
+
+
 def factor_inverse(work, width):
     for start in range(0, width, PANEL):
         stop = start + PANEL
-        left = start // LANES * LANES
-        right = width + (stop + LANES - 1) // LANES * LANES
-        rows = work[start:stop, left:right]
-        index = lax.broadcasted_iota(jnp.int32, (PANEL, 1), 0)
-        diagonal = jnp.zeros((PANEL, 1), F32)
-        for k in range(PANEL):
-            at = start - left + k
-            pivot_row = rows[k : k + 1, :]
-            multiplier = rows[:, at : at + 1]
-            pivot = multiplier[k : k + 1, :]
-            diagonal = jnp.where(index == k, pivot, diagonal)
-            scaled = jnp.where(index > k, multiplier, 0.0) * (1.0 / pivot)
-            rows = rows - scaled * pivot_row
-        rows = rows * (1.0 / jnp.sqrt(diagonal))
-        work[start:stop, left:right] = rows
+        factor_rows(work, start, stop, width)
         if stop < width:
-            update = lax.dot_general(
-                rows[:, : width - left],
-                rows,
-                (((0,), (0,)), ((), ())),
-                precision=HIGHEST,
-                preferred_element_type=F32,
-            )
-            work[stop:width, left:right] = work[stop:width, left:right] - update[stop - left :, :]
+            take_out(work, start, stop, stop, width, width)
 
 
 def kernel(
-    sizes, jac, probes, std, weight, sketch_out, basis_out,
-    std_col, weight_col, stacked, jt, jrecv, fsend, frecv, wbuf,
+    sizes, jac_hbm, probes_hbm, std_hbm, weight_hbm, sketch_out, inverse_out,
+    jac, probes, std, weight, load_sems, std_col, weight_col, stacked, jt, jrecv, fsend, frecv, wbuf,
     gsend, gpair, gchunk, grecv, gfull, work, send_sems, recv_sems,
 ):
-    n_obs, n_flux, scale = sizes
+    n_obs, n_flux = sizes
     blocks, flux_local, probe_count = probes.shape
     obs_local = jac.shape[0]
     width = blocks * probe_count
@@ -107,16 +146,28 @@
     each(1, chips, greet)
     each(0, chips, greet_other)
 
+    loads = [
+        pltpu.make_async_copy(src, dst, load_sems.at[i])
+        for i, (src, dst) in enumerate(
+            ((std_hbm, std), (weight_hbm, weight), (probes_hbm, probes), (jac_hbm, jac))
+        )
+    ]
+    for load in loads:
+        load.start()
+    loads[0].wait()
+    loads[1].wait()
     for s in range(flux_local // LANES):
         part = slice(s * LANES, (s + 1) * LANES)
         std_col[part, :] = column(std[:, part])
     for s in range(obs_local // LANES):
         part = slice(s * LANES, (s + 1) * LANES)
         weight_col[part, :] = column(weight[:, part])
+    loads[2].wait()
     for b in range(blocks):
         stacked[:, b * probe_count : (b + 1) * probe_count] = (
             probes[b].astype(F32) * std_col[...]
         ).astype(BF16)
+    loads[3].wait()
     partial = jnp.dot(jac[...], stacked[...], preferred_element_type=F32)
     fsend[...] = partial.reshape(w_owners, w_rows, width)
     jt[...] = jac[...].T.reshape(n_obs, portion, obs_local)
@@ -230,11 +281,7 @@
         == lax.broadcasted_iota(jnp.int32, (width, width), 1)
     ).astype(F32)
     factor_inverse(work, width)
-    basis = lax.dot_general(
-        sketch_out[...], work[:, width:], (((1,), (1,)), ((), ())),
-        precision=HIGHEST, preferred_element_type=F32,
-    )
-    basis_out[...] = basis * scale
+    inverse_out[...] = work[:, width:]
 
     if w_mine is True:
         wait_bytes(fsend.at[pl.ds(0, w_owners - 1)], send_sems.at[0])
@@ -258,6 +305,15 @@
 
     only(g_mine, g_sent)
     gacross.wait_send()
+
+
+def finish(scale, sketch, inverse, sketch_out, basis_out):
+    sketch_out[...] = sketch[...]
+    basis = lax.dot_general(
+        sketch[...], inverse[...], (((1,), (1,)), ((), ())),
+        precision=HIGHEST, preferred_element_type=F32,
+    )
+    basis_out[...] = basis * scale
 
 
 def body(jacobian, probes, prior_std, obs_weight):
@@ -274,12 +330,17 @@
     scale = math.sqrt(flux_local * n_flux)
     vmem = pl.BlockSpec(memory_space=pltpu.VMEM)
     out = jax.ShapeDtypeStruct((portion, width), F32)
-    return pl.pallas_call(
-        functools.partial(kernel, (n_obs, n_flux, scale)),
-        out_shape=(out, out),
-        in_specs=[vmem] * 4,
+    sketch, inverse = pl.pallas_call(
+        functools.partial(kernel, (n_obs, n_flux)),
+        out_shape=(out, jax.ShapeDtypeStruct((width, width), F32)),
+        in_specs=[pl.BlockSpec(memory_space=pl.ANY)] * 4,
         out_specs=(vmem, vmem),
         scratch_shapes=[
+            pltpu.VMEM(jacobian.shape, BF16),
+            pltpu.VMEM(probes.shape, BF16),
+            pltpu.VMEM((1, flux_local), F32),
+            pltpu.VMEM((1, obs_local), F32),
+            pltpu.SemaphoreType.DMA((4,)),
             pltpu.VMEM((flux_local, LANES), F32),
             pltpu.VMEM((obs_local, LANES), F32),
             pltpu.VMEM((flux_local, width), BF16),
@@ -299,6 +360,12 @@
         ],
         compiler_params=pltpu.CompilerParams(collective_id=0, has_side_effects=True),
     )(jacobian, probes, prior_std.reshape(1, -1), obs_weight.reshape(1, -1))
+    return pl.pallas_call(
+        functools.partial(finish, scale),
+        out_shape=(out, out),
+        in_specs=[vmem] * 2,
+        out_specs=(vmem, vmem),
+    )(sketch, inverse)
 
 
 def solution(mesh):

time: 61.6 us -> 43.1 us (0.70)
  Pallas kernels: 58.4 us -> 42.3 us
  local copies, waits for them, and re-layouts: 2.42 us -> 0 us
    pallas_call x1 -> x2, Pallas kernels: 58.4 us -> 42.3 us  [the longest x1 40.1 us: body(): pl.pallas_call(functools.partial(kernel, (n_obs, n_flux)), out_shape=(out...]
    unnamed x4 -> x0, local copies, waits for them, and re-layouts: 2.42 us -> none
where the time goes in v2:
time: 43.1 us; the launch traced here: 42.9 us
  Pallas kernels  42.3 us (98%)
  between operations  0.64 us (1%)
    pallas_call x1, Pallas kernels, body(): pl.pallas_call(functools.partial(kernel, (n_obs, n_flux)), out_shape=(out...  40.1 us
    pallas_call x1, Pallas kernels, body(): pl.pallas_call(functools.partial(finish, scale), out_shape=(out, out), in...  2.17 us

profile of v2, /device:TPU:1, one launch (start us, length us, event | category | flops | bytes accessed | tf_op | source)
XLA Modules:
  0.0 42.9 jit_solution(11630739763109108740)
XLA Ops:
  0.6 40.1 %shard_map.59 = (f32[256,256]{1,0:T(8,128)}, f32[256,256]{1,0:T(8,128)}) custom-call(bf16[128,1024]{1,0:T(8,128)(2,1)} %jac_hbm.1, bf16[2,1024,128]{2,1,0:T(8,128)(2,1)} %probes_hbm.1, f32[1,1024]{1,0:T(1,128)} %bitcast.2, f32[1,128]{1,0:T(1,128)} %bitcast.3), custom_call_target="tpu_custom_call" | custom-call | tf_op jit(solution)/shard_map/pallas_call | solution.py:333
  40.8 2.2 %shard_map.60 = (f32[256,256]{1,0:T(8,128)}, f32[256,256]{1,0:T(8,128)}) custom-call(f32[256,256]{1,0:T(8,128)} %get-tuple-element.4.sketch, f32[256,256]{1,0:T(8,128)} %get-tuple-element.5.inverse), custom_call_target="tpu_custom_call" | custom-call | tf_op jit(solution)/shard_map/pallas_call | solution.py:363

commit v3 on v2

--- a/solution.py
+++ b/solution.py
@@ -99,18 +99,11 @@
     work[low:high, left:right] = work[low:high, left:right] - update[low - left : high - left, :]
 
 
-def factor_inverse(work, width):
-    for start in range(0, width, PANEL):
-        stop = start + PANEL
-        factor_rows(work, start, stop, width)
-        if stop < width:
-            take_out(work, start, stop, stop, width, width)
-
-
 def kernel(
     sizes, jac_hbm, probes_hbm, std_hbm, weight_hbm, sketch_out, inverse_out,
     jac, probes, std, weight, load_sems, std_col, weight_col, stacked, jt, jrecv, fsend, frecv, wbuf,
-    gsend, gpair, gchunk, grecv, gfull, work, send_sems, recv_sems,
+    gsend, gpair, gchunk, grecv, gfull,
+    tsend, tpair, tchunk, trecv, tfull, work, send_sems, recv_sems,
 ):
     n_obs, n_flux = sizes
     blocks, flux_local, probe_count = probes.shape
@@ -237,12 +230,20 @@
     at = pl.ds(pl.multiple_of(o * portion, portion), portion)
     sketch = total * jnp.concatenate([std_col[at, :]] * (width // LANES), axis=1)
     sketch_out[...] = sketch
-    gram = lax.dot_general(
-        sketch, sketch, (((0,), (0,)), ((), ())), precision=HIGHEST, preferred_element_type=F32
-    )
-    gsend[...] = gram.reshape(gsend.shape)
-
+    half = width // 2
+
+    def gram(low, high):
+        return lax.dot_general(
+            sketch[:, low : low + half], sketch[:, high : high + half],
+            (((0,), (0,)), ((), ())), precision=HIGHEST, preferred_element_type=F32,
+        )
+
+    gsend[0] = gram(0, 0).reshape(gsend.shape[1:])
+    gsend[1] = gram(0, half).reshape(gsend.shape[1:])
     pair = send(gsend.at[1 - core], gpair, 4, partner)
+    tsend[...] = gram(half, half).reshape(tsend.shape)
+    tpair_copy = send(tsend.at[1 - core], tpair, 8, partner)
+
     pair.wait_recv()
     gchunk[...] = gsend[core] + gpair[...]
 
@@ -255,6 +256,23 @@
 
     each(1, chips, send_gram)
 
+    tpair_copy.wait_recv()
+    tchunk[...] = tsend[core] + tpair[...]
+    t_owners = tchunk.shape[0]
+    piece = chip // 2
+    t_mine = (chip == 2 * piece + lax.rem(piece, 2)) & (piece < t_owners)
+
+    def send_tail(step):
+        owned = lax.rem(piece + step, t_owners)
+        owner = 2 * owned + lax.rem(owned, 2)
+        device = ((owner // n_flux) * 2 + core, lax.rem(owner, n_flux))
+        only(
+            owner != chip,
+            lambda: send(tchunk.at[owned], trecv.at[chip], 9, device) and None,
+        )
+
+    each(0, t_owners, send_tail)
+
     def total_gram():
         grecv[chip] = gchunk[chip]
         wait_bytes(grecv.at[pl.ds(0, chips - 1)], recv_sems.at[5])
@@ -267,20 +285,47 @@
         each(1, chips, share)
 
     only(g_mine, total_gram)
+    work[:, width:] = (
+        lax.broadcasted_iota(jnp.int32, (width, width), 0)
+        == lax.broadcasted_iota(jnp.int32, (width, width), 1)
+    ).astype(F32)
+
+    def total_tail():
+        trecv[chip] = tchunk[piece]
+        wait_bytes(trecv.at[pl.ds(0, chips - 1)], recv_sems.at[9])
+        tfull[core * t_owners + piece] = jnp.sum(trecv[...], axis=0)
+
+        def share(step, c):
+            _, device = on_chip(step, c)
+            send(tfull.at[core * t_owners + piece], tfull.at[core * t_owners + piece], 10, device)
+
+        each(1, chips, lambda step: share(step, core))
+        each(0, chips, lambda step: share(step, 1 - core))
+
     if g_mine is True:
         wait_bytes(gfull.at[core, pl.ds(0, g_owners - 1)], recv_sems.at[6])
     else:
         pl.when(g_mine)(lambda: wait_bytes(gfull.at[core, pl.ds(0, g_owners - 1)], recv_sems.at[6]))
         pl.when(chip >= g_owners)(lambda: wait_bytes(gfull.at[core], recv_sems.at[6]))
     gacross = send(gfull.at[core], gfull.at[core], 7, partner)
+    only(t_mine, total_tail)
     gacross.wait_recv()
 
-    work[:, :width] = gfull[...].reshape(width, width)
-    work[:, width:] = (
-        lax.broadcasted_iota(jnp.int32, (width, width), 0)
-        == lax.broadcasted_iota(jnp.int32, (width, width), 1)
-    ).astype(F32)
-    factor_inverse(work, width)
+    work[:half, :half] = gfull[0].reshape(half, half)
+    work[:half, half:width] = gfull[1].reshape(half, half)
+    for start in range(0, half, PANEL):
+        factor_rows(work, start, start + PANEL, width)
+        if start + PANEL < half:
+            take_out(work, start, start + PANEL, start + PANEL, half, width)
+
+    pl.when(t_mine)(lambda: wait_bytes(tfull.at[pl.ds(0, 2 * t_owners - 1)], recv_sems.at[10]))
+    pl.when(jnp.logical_not(t_mine))(lambda: wait_bytes(tfull, recv_sems.at[10]))
+    work[half:, half:width] = tfull[...].reshape(half, half)
+    take_out(work, 0, half, half, width, width)
+    for start in range(half, width, PANEL):
+        factor_rows(work, start, start + PANEL, width)
+        if start + PANEL < width:
+            take_out(work, start, start + PANEL, start + PANEL, width, width)
     inverse_out[...] = work[:, width:]
 
     if w_mine is True:
@@ -305,6 +350,16 @@
 
     only(g_mine, g_sent)
     gacross.wait_send()
+    tpair_copy.wait_send()
+
+    def tail_sent(count):
+        each(0, count, lambda step: wait_bytes(tchunk.at[0], send_sems.at[9]))
+
+    pl.when(t_mine)(lambda: tail_sent(t_owners - 1))
+    pl.when(jnp.logical_not(t_mine))(lambda: tail_sent(t_owners))
+    pl.when(t_mine)(
+        lambda: each(1, 2 * chips, lambda step: wait_bytes(tchunk.at[0], send_sems.at[10]))
+    )
 
 
 def finish(scale, sketch, inverse, sketch_out, basis_out):
@@ -325,8 +380,10 @@
     chips = n_obs // 2 * n_flux
     w_rows = max(16, obs_local // n_flux)
     w_owners = obs_local // w_rows
-    g_rows = max(8, width // 2 // chips)
-    g_owners = width // 2 // g_rows
+    half = width // 2
+    g_rows = max(TILE, half // chips)
+    g_owners = half // g_rows
+    t_owners = half // 2 // TILE
     scale = math.sqrt(flux_local * n_flux)
     vmem = pl.BlockSpec(memory_space=pltpu.VMEM)
     out = jax.ShapeDtypeStruct((portion, width), F32)
@@ -349,14 +406,19 @@
             pltpu.VMEM((w_owners, w_rows, width), F32),
             pltpu.VMEM((n_flux, w_rows, width), F32),
             pltpu.VMEM((2, n_obs // 2 * w_owners, w_rows, width), BF16),
-            pltpu.VMEM((2, g_owners, g_rows, width), F32),
-            pltpu.VMEM((g_owners, g_rows, width), F32),
-            pltpu.VMEM((g_owners, g_rows, width), F32),
-            pltpu.VMEM((chips, g_rows, width), F32),
-            pltpu.VMEM((2, g_owners, g_rows, width), F32),
+            pltpu.VMEM((2, g_owners, g_rows, half), F32),
+            pltpu.VMEM((g_owners, g_rows, half), F32),
+            pltpu.VMEM((g_owners, g_rows, half), F32),
+            pltpu.VMEM((chips, g_rows, half), F32),
+            pltpu.VMEM((2, g_owners, g_rows, half), F32),
+            pltpu.VMEM((2, t_owners, TILE, half), F32),
+            pltpu.VMEM((t_owners, TILE, half), F32),
+            pltpu.VMEM((t_owners, TILE, half), F32),
+            pltpu.VMEM((chips, TILE, half), F32),
+            pltpu.VMEM((2 * t_owners, TILE, half), F32),
             pltpu.VMEM((width, 2 * width), F32),
-            pltpu.SemaphoreType.DMA((8,)),
-            pltpu.SemaphoreType.DMA((8,)),
+            pltpu.SemaphoreType.DMA((11,)),
+            pltpu.SemaphoreType.DMA((11,)),
         ],
         compiler_params=pltpu.CompilerParams(collective_id=0, has_side_effects=True),
     )(jacobian, probes, prior_std.reshape(1, -1), obs_weight.reshape(1, -1))

time: 43.1 us -> 42.3 us (0.981)
  Pallas kernels: 42.3 us -> 41.5 us
    pallas_call x1, Pallas kernels: 40.1 us -> 39.4 us  [body(): pl.pallas_call(functools.partial(kernel, (n_obs, n_flux)), out_shape=(out...]
where the time goes in v3:
time: 42.3 us; the launch traced here: 42.2 us
  Pallas kernels  41.5 us (98%)
  between operations  0.64 us (2%)
    pallas_call x1, Pallas kernels, body(): pl.pallas_call(functools.partial(kernel, (n_obs, n_flux)), out_shape=(out...  39.4 us
    pallas_call x1, Pallas kernels, body(): pl.pallas_call(functools.partial(finish, scale), out_shape=(out, out), in...  2.17 us

profile of v3, /device:TPU:1, one launch (start us, length us, event | category | flops | bytes accessed | tf_op | source)
XLA Modules:
  0.0 42.2 jit_solution(4586972491815488976)
XLA Ops:
  0.6 39.4 %shard_map.59 = (f32[256,256]{1,0:T(8,128)}, f32[256,256]{1,0:T(8,128)}) custom-call(bf16[128,1024]{1,0:T(8,128)(2,1)} %jac_hbm.1, bf16[2,1024,128]{2,1,0:T(8,128)(2,1)} %probes_hbm.1, f32[1,1024]{1,0:T(1,128)} %bitcast.2, f32[1,128]{1,0:T(1,128)} %bitcast.3), custom_call_target="tpu_custom_call" | custom-call | tf_op jit(solution)/shard_map/pallas_call | solution.py:390
  40.0 2.2 %shard_map.60 = (f32[256,256]{1,0:T(8,128)}, f32[256,256]{1,0:T(8,128)}) custom-call(f32[256,256]{1,0:T(8,128)} %get-tuple-element.4.sketch, f32[256,256]{1,0:T(8,128)} %get-tuple-element.5.inverse), custom_call_target="tpu_custom_call" | custom-call | tf_op jit(solution)/shard_map/pallas_call | solution.py:425

commit v4 on v3

--- a/solution.py
+++ b/solution.py
@@ -15,6 +15,7 @@
 LANES = 128
 PANEL = 64
 TILE = 8
+VMEM_LIMIT = 24 * 2**20
 
 
 def each(lower, upper, step):
@@ -390,7 +391,7 @@
     sketch, inverse = pl.pallas_call(
         functools.partial(kernel, (n_obs, n_flux)),
         out_shape=(out, jax.ShapeDtypeStruct((width, width), F32)),
-        in_specs=[pl.BlockSpec(memory_space=pl.ANY)] * 4,
+        in_specs=[pl.BlockSpec(memory_space=pltpu.HBM)] * 4,
         out_specs=(vmem, vmem),
         scratch_shapes=[
             pltpu.VMEM(jacobian.shape, BF16),
@@ -420,13 +421,16 @@
             pltpu.SemaphoreType.DMA((11,)),
             pltpu.SemaphoreType.DMA((11,)),
         ],
-        compiler_params=pltpu.CompilerParams(collective_id=0, has_side_effects=True),
+        compiler_params=pltpu.CompilerParams(
+            collective_id=0, has_side_effects=True, vmem_limit_bytes=VMEM_LIMIT
+        ),
     )(jacobian, probes, prior_std.reshape(1, -1), obs_weight.reshape(1, -1))
     return pl.pallas_call(
         functools.partial(finish, scale),
         out_shape=(out, out),
         in_specs=[vmem] * 2,
         out_specs=(vmem, vmem),
+        compiler_params=pltpu.CompilerParams(vmem_limit_bytes=VMEM_LIMIT),
     )(sketch, inverse)
 
 

time: 42.3 us -> 43.6 us (1.031)
  local copies, waits for them, and re-layouts: 0 us -> 3.33 us
  Pallas kernels: 41.5 us -> 39.4 us
    unnamed x0 -> x8, local copies, waits for them, and re-layouts: none -> 3.33 us
    pallas_call x1, Pallas kernels: 39.4 us -> 38.3 us  [body(): pl.pallas_call(functools.partial(kernel, (n_obs, n_flux)), out_shape=(out...]
    pallas_call x1, Pallas kernels: 2.17 us -> 1.14 us  [body(): pl.pallas_call(functools.partial(finish, scale), out_shape=(out, out), in...]
where the time goes in v4:
time: 43.6 us; the launch traced here: 43.4 us
  Pallas kernels  39.4 us (90%)
  local copies, waits for them, and re-layouts  3.33 us (8%)
  between operations  0.65 us (1%)
    pallas_call x1, Pallas kernels, body(): pl.pallas_call(functools.partial(kernel, (n_obs, n_flux)), out_shape=(out...  38.3 us
    unnamed x8, local copies, waits for them, and re-layouts  3.33 us
    pallas_call x1, Pallas kernels, body(): pl.pallas_call(functools.partial(finish, scale), out_shape=(out, out), in...  1.14 us

profile of v4, /device:TPU:1, one launch (start us, length us, event | category | flops | bytes accessed | tf_op | source)
XLA Modules:
  0.0 43.4 jit_solution(13100422544231508805)
XLA Ops:
  0.6 0.0 copy-start.3
  0.6 0.6 %copy-done.3 = f32[128]{0:T(128)S(1)} copy-done((f32[128]{0:T(128)S(1)}, f32[128]{0:T(128)}, u32[]{:S(2)}) %copy-start.3) | copy-done | bytes 536
  1.3 0.0 copy-start
  1.3 1.0 %copy-done = bf16[2,1024,128]{2,1,0:T(8,128)(2,1)S(1)} copy-done((bf16[2,1024,128]{2,1,0:T(8,128)(2,1)S(1)}, bf16[2,1024,128]{2,1,0:T(8,128)(2,1)}, u32[]{:S(2)}) %copy-start) | copy-done | bytes 524312
  2.3 0.0 copy-start.1
  2.3 0.9 %copy-done.1 = bf16[128,1024]{1,0:T(8,128)(2,1)S(1)} copy-done((bf16[128,1024]{1,0:T(8,128)(2,1)S(1)}, bf16[128,1024]{1,0:T(8,128)(2,1)}, u32[]{:S(2)}) %copy-start.1) | copy-done | bytes 262168
  3.3 0.0 copy-start.2
  3.3 0.7 %copy-done.2 = f32[1024]{0:T(1024)S(1)} copy-done((f32[1024]{0:T(1024)S(1)}, f32[1024]{0:T(1024)}, u32[]{:S(2)}) %copy-start.2) | copy-done | bytes 4120
  4.0 38.3 %shard_map.59 = (f32[256,256]{1,0:T(8,128)S(1)}, f32[256,256]{1,0:T(8,128)S(1)}) custom-call(bf16[128,1024]{1,0:T(8,128)(2,1)S(1)} %copy-done.1, bf16[2,1024,128]{2,1,0:T(8,128)(2,1)S(1)} %copy-done, f32[1,1024]{1,0:T(1,128)S(1)} %bitcast.2, f32[1,128]{1,0:T(1,128)S(1)} %bitcast.3), custom_call_target="tpu_custom_call" | custom-call | tf_op jit(solution)/shard_map/pallas_call | solution.py:391
  42.3 1.1 %shard_map.60 = (f32[256,256]{1,0:T(8,128)}, f32[256,256]{1,0:T(8,128)}) custom-call(f32[256,256]{1,0:T(8,128)S(1)} %get-tuple-element.4.sketch, f32[256,256]{1,0:T(8,128)S(1)} %get-tuple-element.5.inverse), custom_call_target="tpu_custom_call" | custom-call | tf_op jit(solution)/shard_map/pallas_call | solution.py:428
Async XLA Ops:
  0.6 0.7 %copy-start.3 = (f32[128]{0:T(128)S(1)}, f32[128]{0:T(128)}, u32[]{:S(2)}) copy-start(f32[128]{0:T(128)} %param.7) | copy-start | bytes 1540
  1.3 1.0 %copy-start = (bf16[2,1024,128]{2,1,0:T(8,128)(2,1)S(1)}, bf16[2,1024,128]{2,1,0:T(8,128)(2,1)}, u32[]{:S(2)}) copy-start(bf16[2,1024,128]{2,1,0:T(8,128)(2,1)} %probes_hbm.1) | copy-start | bytes 1572868
  2.3 0.9 %copy-start.1 = (bf16[128,1024]{1,0:T(8,128)(2,1)S(1)}, bf16[128,1024]{1,0:T(8,128)(2,1)}, u32[]{:S(2)}) copy-start(bf16[128,1024]{1,0:T(8,128)(2,1)} %jac_hbm.1) | copy-start | bytes 786436
  3.3 0.7 %copy-start.2 = (f32[1024]{0:T(1024)S(1)}, f32[1024]{0:T(1024)}, u32[]{:S(2)}) copy-start(f32[1024]{0:T(1024)} %param.6) | copy-start | bytes 12292
